TPU v7x, 128 devices: a whole 4x4x4 slice. The times are simulated.
128 devices in a mesh: row: 8 (over x, core), blk: 16 (over z, y).
Axes of the slice: x: 4, y: 4, z: 4, core: 2. Of those that a mesh axis runs over, the one named last changes fastest.
Arguments:
- panel: float32 [256, 524288], P(None, ('row', 'blk'))
- logits: float32 [524288], P(('row', 'blk')), may hold values from -6 to 6
- signs: int32 [524288], P(('row', 'blk')), may hold values from -1 to 1, as said below
- samples: int32 [128, 96], P(('row', 'blk')), may hold values from 0 to 4095, as said below
- counts: int32 [128], P(('row', 'blk')), may hold values from 32 to 96, as said below
Outputs:
- conditioned: float32 [256, 524288], P(None, ('row', 'blk'))
Inputs may be any that keep to these rules, and one draw needn't show every extreme that they name: `signs`: each entry is -1 or 1. Entry [e, s] names frequency e + 128 * samples[e, s]; an offset may repeat within a row. Row e of samples uses its first counts[e] slots; the others are ignored.
All inputs are finite; a program needn't handle non-finite values.
Results may differ from a plain program's by a relative error of at most 0.000052.
Values sent between devices are 32-bit elements; how exact they have to be, the bound alone decides.
No kernel may reach another device: no remote copies, remote signals or barrier semaphores. Data moves between devices by JAX's collectives and lax.ppermute only.
A program may use at most 128 MiB of HBM per device.

v0:
```python
import functools
import math

import jax
import jax.numpy as jnp
from jax import lax
from jax.experimental import pallas as pl
from jax.experimental.pallas import tpu as pltpu
from jax.sharding import PartitionSpec as P

AXES = ("row", "blk")
LANES = 128
highest = lax.Precision.HIGHEST
f32 = jnp.float32
bf16 = jnp.bfloat16


def split_two(value):
    high = value.astype(bf16)
    low = (value - high.astype(f32)).astype(bf16)
    return high, low


def rounded_parts(value):
    high = lax.reduce_precision(value, 8, 7)
    return high.astype(bf16), (value - high).astype(bf16)


def cos_turns(numerator, length):
    return jnp.cos((2.0 * math.pi / length) * (numerator % length).astype(f32))


def swap_eight(tiles):
    tiles = list(tiles)
    line = lax.broadcasted_iota(jnp.int32, tiles[0].shape, 0)
    for d in (4, 2, 1):
        low = (line & d) == 0
        for i in range(8):
            if i & d == 0:
                first, second = tiles[i], tiles[i + d]
                tiles[i] = jnp.where(low, first, pltpu.roll(second, d, 0))
                tiles[i + d] = jnp.where(low, pltpu.roll(first, 8 - d, 0), second)
    return tiles


def pack_kernel(panel_ref, scale_ref, samples_ref, out_ref):
    lines = panel_ref.shape[0]
    groups = panel_ref.shape[1] // LANES
    for top in range(0, lines, 8):
        for g in range(0, groups, 8):
            spans = [slice((g + i) * LANES, (g + i + 1) * LANES) for i in range(8)]
            tiles = swap_eight([panel_ref[top : top + 8, span] * scale_ref[:, span] for span in spans])
            for i in range(8):
                line = top + i
                row = (line % 2) * groups + g
                out_ref[line // 2, row : row + 8, :] = tiles[i]
    riders = jnp.broadcast_to(samples_ref[...].astype(f32), (8, LANES))
    for q in range(lines // 2):
        out_ref[q, 2 * groups : 2 * groups + 8, :] = riders


def pack(panel, scale, samples):
    columns, rows = panel.shape
    groups = rows // LANES
    step = 32
    return pl.pallas_call(
        pack_kernel,
        grid=(columns // step,),
        in_specs=[
            pl.BlockSpec((step, rows), lambda i: (i, 0)),
            pl.BlockSpec((1, rows), lambda i: (0, 0)),
            pl.BlockSpec((1, LANES), lambda i: (0, 0)),
        ],
        out_specs=pl.BlockSpec((step // 2, 2 * groups + 8, LANES), lambda i: (i, 0, 0)),
        out_shape=jax.ShapeDtypeStruct((columns // 2, 2 * groups + 8, LANES), f32),
        name="pack_columns",
    )(panel, scale, samples)


def unit_circle(step, log_length):
    quarter = log_length - 2
    turn = (step + (1 << (quarter - 1))) >> quarter
    x = (step - (turn << quarter)).astype(f32) * (2.0 * math.pi / (1 << log_length))
    x2 = x * x
    sine = x + x * x2 * (-1 / 6 + x2 * (1 / 120 + x2 * (-1 / 5040 + x2 * (1 / 362880))))
    cosine = 1.0 + x2 * (-0.5 + x2 * (1 / 24 + x2 * (-1 / 720 + x2 * (1 / 40320))))
    odd = (turn & 1) == 1
    a, b = jnp.where(odd, sine, cosine), jnp.where(odd, cosine, sine)
    return jnp.where(((turn + 1) & 2) != 0, -a, a), jnp.where((turn & 2) != 0, -b, b)


def sample_phases(frequency, log_length):
    line = lax.broadcasted_iota(jnp.int32, (8, LANES), 0)
    last = (1 << log_length) - 1
    eighth = 1 << (log_length - 3)
    c2, s2 = unit_circle((frequency * line - eighth) & last, log_length)
    c2, s2 = c2 * math.sqrt(2.0), s2 * math.sqrt(2.0)
    res, ims = [], []
    for half in range(2):
        c8, s8 = unit_circle((frequency * (8 * line + 64 * half)) & last, log_length)
        for a in range(8):
            c1, s1 = c8[a : a + 1], s8[a : a + 1]
            res.append(c1 * c2 - s1 * s2)
            ims.append(c1 * s2 + s1 * c2)
    return jnp.concatenate(res + ims, axis=0)


def middle_table(zero):
    shape = (64, 2, 2, 32, 2, 32)
    p, cls, part, s1, c, ib = (lax.broadcasted_iota(jnp.int32, shape, k) for k in range(6))
    p = p + zero
    e = jnp.where(cls == 0, p, jnp.where(p == 0, 64, 128 - p))
    angle = ib * (e + 128 * s1)
    quarters = jnp.where(cls == 0, part + c, jnp.where(p == 0, part, jnp.where(c == 0, part, 3 * (1 - part))))
    value = cos_turns(angle + 1024 * quarters, 4096)
    value = jnp.where((p == 0) & (c != cls), 0.0, value)
    return value.reshape(64, 128, 64)


def times(value, turn):
    re, im = value
    turn = turn % 1.0
    if turn == 0.0:
        return re, im
    c, s = math.cos(2.0 * math.pi * turn), math.sin(2.0 * math.pi * turn)
    if turn == 0.25:
        return (None if im is None else -im), re
    if turn == 0.5:
        return -re, (None if im is None else -im)
    if im is None:
        return re * c, re * s
    if turn in (0.125, 0.375, 0.625, 0.875):
        root = math.sqrt(0.5)
        plus, minus = (re + im) * root, (re - im) * root
        if turn == 0.125:
            return minus, plus
        if turn == 0.375:
            return -plus, minus
        if turn == 0.625:
            return -minus, -plus
        return plus, -minus
    return re * c - im * s, re * s + im * c


def add(a, b):
    return tuple(y if x is None else (x if y is None else x + y) for x, y in zip(a, b))


def sub(a, b):
    return tuple((None if y is None else -y) if x is None else (x if y is None else x - y) for x, y in zip(a, b))


def small_dft(values):
    length = len(values)
    if length == 1:
        return values
    even, odd = small_dft(values[0::2]), small_dft(values[1::2])
    turned = [times(odd[k], k / length) for k in range(length // 2)]
    return [add(even[k], turned[k]) for k in range(length // 2)] + [sub(even[k], turned[k]) for k in range(length // 2)]


def block_dft(data_ref, y_ref, top):
    inner = [small_dft([(data_ref[16 * n + m], None) for n in range(8)]) for m in range(16)]
    for r in range(5):
        outs = small_dft([times(inner[m][r], m * r / 128) for m in range(16)])
        for f in range(16):
            e = r + 8 * f
            re, im = outs[f]
            if e in (0, 64):
                y_ref[e // 64, pl.ds(top, 8), :] = re
            elif e < 64:
                y_ref[2 * e, pl.ds(top, 8), :] = re
                y_ref[2 * e + 1, pl.ds(top, 8), :] = im
            elif r in (1, 2, 3):
                y_ref[2 * (128 - e), pl.ds(top, 8), :] = re
                y_ref[2 * (128 - e) + 1, pl.ds(top, 8), :] = -im


DATA_STEPS = 8


def transform_kernel(data_ref, rider_ref, middle_ref, out_ref, y_ref, *, log_length):
    step = pl.program_id(0)
    pairs = middle_ref.shape[0]

    @pl.when(step < DATA_STEPS)
    def _():
        block_dft(data_ref, y_ref, pl.multiple_of(step * 8, 8))

    @pl.when(step >= DATA_STEPS)
    def _():
        for q in range(pairs):
            pair = (step - DATA_STEPS) * pairs + q
            cosines = y_ref[2 * pair]
            sines = y_ref[2 * pair + 1]
            stack = jnp.concatenate(
                [
                    jnp.concatenate([cosines[:32], cosines[32:]], axis=1),
                    jnp.concatenate([sines[:32], sines[32:]], axis=1),
                ],
                axis=0,
            )
            hi, lo = split_two(stack)
            mid = middle_ref[q]
            z = jnp.dot(
                jnp.concatenate([mid, mid[:, :64]], axis=1),
                jnp.concatenate([hi, hi, lo], axis=0),
                preferred_element_type=f32,
            )
            for cls in range(2):
                zr = z[cls * 64 : cls * 64 + 32]
                zi = z[cls * 64 + 32 : cls * 64 + 64]
                left = jnp.concatenate(
                    [
                        jnp.concatenate([zr[:, :128], zi[:, :128]], axis=1),
                        jnp.concatenate([zr[:, 128:], zi[:, 128:]], axis=1),
                    ],
                    axis=0,
                )
                hi, lo = split_two(left)
                if cls == 0:
                    e = pair
                else:
                    e = jnp.where(pair == 0, 64, 128 - pair)
                offset = rider_ref[e].astype(jnp.int32)
                t_hi, t_lo = split_two(sample_phases(offset * 128 + e, log_length))
                both = jnp.dot(
                    jnp.concatenate([hi, lo], axis=0),
                    jnp.concatenate([t_hi, t_lo], axis=1),
                    preferred_element_type=f32,
                )
                res = both[:64, :LANES] + both[64:, :LANES] + both[:64, LANES:]
                wanted = jnp.concatenate([offset & 31] * 4, axis=0)
                mask = lax.broadcasted_iota(jnp.int32, (32, LANES), 0) == wanted
                first = jnp.sum(jnp.where(mask, res[:32], 0.0), axis=0, keepdims=True)
                second = jnp.sum(jnp.where(mask, res[32:], 0.0), axis=0, keepdims=True)
                out_ref[e] = jnp.concatenate([first, second], axis=0)


def transform(data, middle, total_rows):
    pairs = 8
    return pl.pallas_call(
        functools.partial(transform_kernel, log_length=total_rows.bit_length() - 1),
        grid=(DATA_STEPS + 64 // pairs,),
        in_specs=[
            pl.BlockSpec((128, 8, LANES), lambda i: (0, jnp.minimum(i, DATA_STEPS - 1), 0)),
            pl.BlockSpec((128, 8, LANES), lambda i: (0, DATA_STEPS, 0)),
            pl.BlockSpec((pairs, 128, 128), lambda i: (jnp.maximum(i - DATA_STEPS, 0), 0, 0)),
        ],
        out_specs=pl.BlockSpec((128, 2, LANES), lambda i: (0, 0, 0)),
        out_shape=jax.ShapeDtypeStruct((128, 2, LANES), f32),
        scratch_shapes=[pltpu.VMEM((128, 64, LANES), f32)],
        compiler_params=pltpu.CompilerParams(vmem_limit_bytes=48 * 1024 * 1024),
        name="sampled_transform",
    )(data, data, middle)


def factor_inverse(a_ref, b_ref):
    size = a_ref.shape[0]
    block = 32
    line = lax.broadcasted_iota(jnp.int32, (8, LANES), 0)
    spread = lambda row: jnp.broadcast_to(row, (8, LANES))
    for lo in range(0, size, block):
        home = lo // LANES
        off = lo % LANES
        spots = [(a_ref, g) for g in range(home, size // LANES)] + [(b_ref, g) for g in range(home + 1)]
        rows = [[ref[lo + 8 * v : lo + 8 * v + 8, g * LANES : (g + 1) * LANES] for ref, g in spots] for v in range(4)]
        pivots = []
        for t in range(4):
            col = [
                {v: jnp.broadcast_to(rows[v][0][:, off + 8 * t + j : off + 8 * t + j + 1], (8, LANES)) for v in range(t, 4)}
                for j in range(8)
            ]
            diag = jnp.ones((8, LANES), f32)
            for j in range(8):
                pivot = spread(col[j][t][j : j + 1])
                inverse = 1.0 / pivot
                diag = jnp.where(line == j, pivot, diag)
                mult = {v: col[j][v] * inverse for v in range(t, 4)}
                mult[t] = jnp.where(line > j, mult[t], 0.0)
                for n in range(j + 1, 8):
                    across = spread(col[j][t][n : n + 1])
                    for v in range(t, 4):
                        col[n][v] = col[n][v] - mult[v] * across
                for g in range(len(spots)):
                    across = spread(rows[t][g][j : j + 1])
                    for v in range(t, 4):
                        rows[v][g] = rows[v][g] - mult[v] * across
            pivots.append(diag)
        for v in range(4):
            scale = lax.rsqrt(pivots[v])
            scale = scale * (1.5 - 0.5 * (pivots[v] * scale) * scale)
            rows[v] = [part * scale for part in rows[v]]
        n_a = size // LANES - home
        for v in range(4):
            for g in range(home + 1):
                b_ref[lo + 8 * v : lo + 8 * v + 8, g * LANES : (g + 1) * LANES] = rows[v][n_a + g]
        if lo + block == size:
            break
        whole = jnp.concatenate([jnp.concatenate(parts, axis=1) for parts in rows], axis=0)
        turned = whole[:, : n_a * LANES].T
        start = lo + block
        cuts = [start, start + block] + ([size] if start + block < size else [])
        for top, end in zip(cuts[:-1], cuts[1:]):
            first = home * LANES
            change = jnp.dot(turned[top - first : end - first], whole, precision=highest, preferred_element_type=f32)
            a_ref[top:end, first:] = a_ref[top:end, first:] - change[:, : n_a * LANES]
            b_ref[top:end, : (home + 1) * LANES] = b_ref[top:end, : (home + 1) * LANES] - change[:, n_a * LANES :]


def finish_kernel(gram_ref, root_ref, panel_ref, out_ref, a_ref, b_ref, w_ref, held_ref, sem):
    size = gram_ref.shape[0]
    width = out_ref.shape[1]

    @pl.when(pl.program_id(0) == 0)
    def _():
        fetch = pltpu.make_async_copy(panel_ref, held_ref, sem)
        fetch.start()
        a_ref[...] = gram_ref[...]
        b_ref[...] = (
            lax.broadcasted_iota(jnp.int32, (size, size), 0) == lax.broadcasted_iota(jnp.int32, (size, size), 1)
        ).astype(f32)
        factor_inverse(a_ref, b_ref)
        total = gram_ref[size - 1 : size, 0:1]
        inverse = b_ref[...] * jnp.sqrt(total)
        high, low = split_two(inverse)
        w_ref[:, :size] = high
        w_ref[:, size : 2 * size] = high
        w_ref[:, 2 * size :] = low
        fetch.wait()

    span = pl.ds(pl.multiple_of(pl.program_id(0) * width, width), width)
    high, low = split_two(held_ref[:, span] * root_ref[...])
    out_ref[...] = jnp.dot(w_ref[...], jnp.concatenate([high, low, high], axis=0), preferred_element_type=f32)


def finish(gram, root_weight, panel):
    columns, rows = panel.shape
    width = 512
    return pl.pallas_call(
        finish_kernel,
        grid=(rows // width,),
        in_specs=[
            pl.BlockSpec((columns, columns), lambda i: (0, 0)),
            pl.BlockSpec((1, width), lambda i: (0, i)),
            pl.BlockSpec(memory_space=pl.ANY),
        ],
        out_specs=pl.BlockSpec((columns, width), lambda i: (0, i)),
        out_shape=jax.ShapeDtypeStruct((columns, rows), f32),
        scratch_shapes=[
            pltpu.VMEM((columns, columns), f32),
            pltpu.VMEM((columns, columns), f32),
            pltpu.VMEM((columns, 3 * columns), bf16),
            pltpu.VMEM((columns, rows), f32),
            pltpu.SemaphoreType.DMA,
        ],
        compiler_params=pltpu.CompilerParams(vmem_limit_bytes=48 * 1024 * 1024),
        name="factor_and_apply",
    )(gram, root_weight, pltpu.with_memory_space_constraint(panel, pltpu.HBM))


def on_device(panel, logits, signs, samples, counts):
    columns, rows_dev = panel.shape
    shards = 128
    total_rows = rows_dev * shards
    slots = samples.shape[1]
    probability = jax.nn.sigmoid(logits)
    root_weight = jnp.sqrt(probability * (1.0 - probability))
    packed = pack(
        panel,
        (root_weight * signs.astype(f32))[None, :],
        jnp.pad(samples, ((0, 0), (0, LANES - slots))),
    )
    arrived = lax.all_to_all(packed, AXES, split_axis=0, concat_axis=0, tiled=True)

    zero = jnp.minimum(counts[0], 0)
    m_hi, m_lo = rounded_parts(middle_table(zero))
    middle = jnp.concatenate([m_hi, m_lo], axis=2)

    picked = transform(arrived, middle, total_rows)
    mine = lax.all_to_all(picked, AXES, split_axis=0, concat_axis=0, tiled=True).reshape(columns, LANES)
    live = jnp.arange(LANES, dtype=jnp.int32)[None, :] < counts[0]
    sketch = jnp.where(live, mine * (1.0 / math.sqrt(total_rows)), 0.0)
    gram_part = jnp.dot(sketch, sketch.T, precision=highest)
    corner = (jnp.arange(columns)[:, None] == columns - 1) & (jnp.arange(columns)[None, :] == 0)
    gram_part = jnp.where(corner, counts[0].astype(f32), gram_part)
    lines = columns // shards
    strips = lax.all_to_all(
        gram_part.reshape(shards, lines, columns), AXES, split_axis=0, concat_axis=0, tiled=True
    ).sum(0)
    gram = lax.all_to_all(
        jnp.broadcast_to(strips[None], (shards, lines, columns)), AXES, split_axis=0, concat_axis=0, tiled=True
    ).reshape(columns, columns)
    return finish(gram, root_weight[None, :], panel)


def solution(mesh):
    placed = (
        P(None, AXES),
        P(AXES),
        P(AXES),
        P(AXES, None),
        P(AXES),
    )
    return jax.shard_map(on_device, mesh=mesh, in_specs=placed, out_specs=P(None, AXES), check_vma=False)
```

profile of v0, /device:TPU:1, one launch (start us, length us, event | category | flops | bytes accessed | tf_op | source)
XLA Modules:
  0.0 161.0 jit_solution(17717346733335143452)
XLA Ops:
  0.0 1.4 fusion.6
  1.4 1.2 pad.4.samples_ref
  2.6 7.1 %pack_columns.1 = f32[128,72,128]{2,1,0:T(8,128)} custom-call(f32[256,4096]{1,0:T(8,128)} %panel_ref.3, f32[1,4096]{1,0:T(1,128)} %bitcast.11, s32[1,128]{1,0:T(1,128)} %pad.4.samples_ref), custom_call_target="tpu_custom_call" | custom-call | tf_op jit(solution)/shard_map/pack_columns/pallas_call | solution.py:66
  9.6 11.9 %all-to-all-start = ((f32[128,72,128]{2,1,0:T(8,128)}), f32[128,72,128]{2,1,0:T(8,128)}, u32[]{:S(2)}, u32[]{:S(2)}) async-start(f32[128,72,128]{2,1,0:T(8,128)} %pack_columns.1), calls=%async_computation | async-start | bytes 9437184 | tf_op jit(solution)/shard_map/all_to_all | solution.py:374
  21.5 0.1 iota.157
  21.6 0.1 iota.158
  21.7 0.1 iota.153
  21.8 0.1 iota.154
  21.9 0.1 iota.151
  22.0 0.1 iota.148
  22.7 0.1 iota.141
  22.8 0.1 iota.142
  22.9 0.1 iota.138
  23.0 0.1 iota.135
  23.0 0.1 iota.132
  23.1 17.3 %reduce-precision_convert_fusion = (bf16[64,128,64]{2,1,0:T(8,128)(2,1)S(1)}, bf16[64,128,64]{2,1,0:T(8,128)(2,1)S(1)}) fusion(s32[128]{0:T(128)S(1)} %iota.158, pred[64]{0:T(512)(128)(4,1)S(1)} %iota.154, s32[128]{0:T(128)S(1)} %iota.151, s32[128]{0:T(128)S(1)} %iota.148, s32[64]{0:T(128)S(1)} %get-tuple-element.10, s32[64]{0:T(128)S(1)} %get-tuple-element.9, ...), kind=kLoop, calls=%fused_computation.4 | loop fusion | flops 15728640 | bytes 2100480 | tf_op jit(solution)/shard_map/convert_element_type | solution.py:26
  40.5 1.2 pad_maximum_fusion.middle_ref
  41.6 36.1 %all-to-all-done.data_ref.rider_ref = f32[128,72,128]{2,1,0:T(8,128)} async-done(((f32[128,72,128]{2,1,0:T(8,128)}), f32[128,72,128]{2,1,0:T(8,128)}, u32[]{:S(2)}, u32[]{:S(2)}) %all-to-all-start) | async-done | bytes 4718624 | tf_op jit(solution)/shard_map/all_to_all | solution.py:374
  77.8 19.2 %sampled_transform.1 = f32[128,2,128]{2,1,0:T(2,128)} custom-call(f32[128,72,128]{2,1,0:T(8,128)} %all-to-all-done.data_ref.rider_ref, f32[128,72,128]{2,1,0:T(8,128)} %all-to-all-done.data_ref.rider_ref, bf16[64,128,128]{2,1,0:T(8,128)(2,1)S(1)} %pad_maximum_fusion.middle_ref), custom_call_target="tpu_custom_call" | custom-call | tf_op jit(solution)/shard_map/sampled_transform/pallas_call | solution.py:242
  97.0 6.7 %all-to-all-start.1 = ((f32[128,2,128]{2,1,0:T(2,128)}), f32[128,2,128]{2,1,0:T(2,128)S(1)}, u32[]{:S(2)}, u32[]{:S(2)}) async-start(f32[128,2,128]{2,1,0:T(2,128)} %sampled_transform.1), calls=%async_computation.1 | async-start | bytes 262144 | tf_op jit(solution)/shard_map/all_to_all | solution.py:381
  103.7 10.2 %all-to-all-done.1 = f32[128,2,128]{2,1,0:T(2,128)S(1)} async-done(((f32[128,2,128]{2,1,0:T(2,128)}), f32[128,2,128]{2,1,0:T(2,128)S(1)}, u32[]{:S(2)}, u32[]{:S(2)}) %all-to-all-start.1) | async-done | bytes 131104 | tf_op jit(solution)/shard_map/all_to_all | solution.py:381
  113.8 0.1 multiply_select_fusion
  113.9 0.4 convolution_select_fusion
  114.3 0.1 reshape.48
  114.5 15.3 %all_to_all.20 = f32[128,2,256]{2,1,0:T(2,128)S(1)} all-to-all(f32[128,2,256]{2,1,0:T(2,128)S(1)} %reshape.48), channel_id=1, replica_groups=mesh['row'=8,'blk'=16] {'row','blk'}, dimensions={0} | all-to-all | bytes 524288 | tf_op jit(solution)/shard_map/all_to_all | solution.py:388
  129.7 0.1 reduce_sum.9
  129.9 0.1 broadcast_in_dim.45
  130.0 15.2 %all_to_all.21 = f32[128,2,256]{2,1,0:T(2,128)S(1)} all-to-all(f32[128,2,256]{2,1,0:T(2,128)S(1)} %broadcast_in_dim.45), channel_id=1, replica_groups=mesh['row'=8,'blk'=16] {'row','blk'}, dimensions={0} | all-to-all | bytes 524288 | tf_op jit(solution)/shard_map/all_to_all | solution.py:391
  145.2 0.2 reshape.49.gram_ref
  145.4 15.4 %factor_and_apply.1 = f32[256,4096]{1,0:T(8,128)} custom-call(f32[256,256]{1,0:T(8,128)S(1)} %reshape.49.gram_ref, f32[1,4096]{1,0:T(1,128)S(1)} %bitcast.9, f32[256,4096]{1,0:T(8,128)} %panel_ref.3), custom_call_target="tpu_custom_call" | custom-call | tf_op jit(solution)/shard_map/factor_and_apply/pallas_call | solution.py:340
  (12 shorter events, 0.1 us)
Async XLA Ops:
  9.6 68.2 %all-to-all-start = ((f32[128,72,128]{2,1,0:T(8,128)}), f32[128,72,128]{2,1,0:T(8,128)}, u32[]{:S(2)}, u32[]{:S(2)}) async-start(f32[128,72,128]{2,1,0:T(8,128)} %pack_columns.1), calls=%async_computation | async-start | bytes 9437184 | tf_op jit(solution)/shard_map/all_to_all | solution.py:374
  97.0 16.9 %all-to-all-start.1 = ((f32[128,2,128]{2,1,0:T(2,128)}), f32[128,2,128]{2,1,0:T(2,128)S(1)}, u32[]{:S(2)}, u32[]{:S(2)}) async-start(f32[128,2,128]{2,1,0:T(2,128)} %sampled_transform.1), calls=%async_computation.1 | async-start | bytes 262144 | tf_op jit(solution)/shard_map/all_to_all | solution.py:381
where the time goes:
time: 162 us; the launch traced here: 161 us
  waiting for transfers between devices  46.3 us (29%)
  Pallas kernels  41.6 us (26%)
  blocking collectives  30.5 us (19%)
  other arithmetic  20.1 us (12%)
  starting transfers between devices  18.6 us (11%)
  local copies, waits for them, and re-layouts  2.51 us (2%)
    all_to_all x1, waiting for transfers between devices, on_device(): lax.all_to_all(packed, AXES, split_axis=0, concat_axis=0, tiled=True)  36.1 us
    pallas_call x1, Pallas kernels, transform(): pl.pallas_call(functools.partial(transform_kernel, log_length=total_rows....  19.2 us
    convert_element_type x1, other arithmetic, rounded_parts(): return (high.astype(bf16), (value - high).astype(bf16))  17.3 us
    pallas_call x1, Pallas kernels, finish(): pl.pallas_call(finish_kernel, grid=(rows // width,), in_specs=[pl.BlockSp...  15.4 us
    all_to_all x1, blocking collectives, on_device(): lax.all_to_all(gram_part.reshape(shards, lines, columns), AXES, split_axi...  15.3 us
    all_to_all x1, blocking collectives, on_device(): lax.all_to_all(jnp.broadcast_to(strips[None], (shards, lines, columns)),...  15.2 us
    all_to_all x1, starting transfers between devices, on_device(): lax.all_to_all(packed, AXES, split_axis=0, concat_axis=0, tiled=True)  11.9 us
    all_to_all x1, waiting for transfers between devices, on_device(): lax.all_to_all(picked, AXES, split_axis=0, concat_axis=0, tiled=True)  10.2 us
  transfers between devices with their start and end apart: 2, of which 2 were waited for; matrix products, arithmetic and copies ran while one was open for 12% of the time, Pallas kernels for 0%

commit v1 on v0

--- a/solution.py
+++ b/solution.py
@@ -43,9 +43,20 @@
     return tiles
 
 
-def pack_kernel(panel_ref, scale_ref, samples_ref, out_ref):
+def pack_kernel(panel_ref, logits_ref, signs_ref, samples_ref, out_ref, root_ref, scale_ref, rider_ref):
     lines = panel_ref.shape[0]
     groups = panel_ref.shape[1] // LANES
+    slots = samples_ref.shape[1]
+
+    @pl.when(pl.program_id(0) == 0)
+    def _():
+        probability = 1.0 / (1.0 + jnp.exp(-logits_ref[...]))
+        root = jnp.sqrt(probability * (1.0 - probability))
+        root_ref[...] = root
+        scale_ref[...] = root * signs_ref[...].astype(f32)
+        rider_ref[...] = jnp.zeros_like(rider_ref)
+        rider_ref[:, :slots] = jnp.broadcast_to(samples_ref[...].astype(f32), (8, slots))
+
     for top in range(0, lines, 8):
         for g in range(0, groups, 8):
             spans = [slice((g + i) * LANES, (g + i + 1) * LANES) for i in range(8)]
@@ -54,27 +65,32 @@
                 line = top + i
                 row = (line % 2) * groups + g
                 out_ref[line // 2, row : row + 8, :] = tiles[i]
-    riders = jnp.broadcast_to(samples_ref[...].astype(f32), (8, LANES))
     for q in range(lines // 2):
-        out_ref[q, 2 * groups : 2 * groups + 8, :] = riders
-
-
-def pack(panel, scale, samples):
+        out_ref[q, 2 * groups : 2 * groups + 8, :] = rider_ref[...]
+
+
+def pack(panel, logits, signs, samples):
     columns, rows = panel.shape
     groups = rows // LANES
-    step = 32
+    step = 128
+    whole = pl.BlockSpec((1, rows), lambda i: (0, 0))
     return pl.pallas_call(
         pack_kernel,
         grid=(columns // step,),
         in_specs=[
             pl.BlockSpec((step, rows), lambda i: (i, 0)),
-            pl.BlockSpec((1, rows), lambda i: (0, 0)),
-            pl.BlockSpec((1, LANES), lambda i: (0, 0)),
+            whole,
+            whole,
+            pl.BlockSpec(samples.shape, lambda i: (0, 0)),
         ],
-        out_specs=pl.BlockSpec((step // 2, 2 * groups + 8, LANES), lambda i: (i, 0, 0)),
-        out_shape=jax.ShapeDtypeStruct((columns // 2, 2 * groups + 8, LANES), f32),
+        out_specs=[pl.BlockSpec((step // 2, 2 * groups + 8, LANES), lambda i: (i, 0, 0)), whole],
+        out_shape=[
+            jax.ShapeDtypeStruct((columns // 2, 2 * groups + 8, LANES), f32),
+            jax.ShapeDtypeStruct((1, rows), f32),
+        ],
+        scratch_shapes=[pltpu.VMEM((1, rows), f32), pltpu.VMEM((8, LANES), f32)],
         name="pack_columns",
-    )(panel, scale, samples)
+    )(panel, logits, signs, samples)
 
 
 def unit_circle(step, log_length):
@@ -159,8 +175,8 @@
     return [add(even[k], turned[k]) for k in range(length // 2)] + [sub(even[k], turned[k]) for k in range(length // 2)]
 
 
-def block_dft(data_ref, y_ref, top):
-    inner = [small_dft([(data_ref[16 * n + m], None) for n in range(8)]) for m in range(16)]
+def block_dft(data_ref, part, y_ref, top):
+    inner = [small_dft([(data_ref[16 * n + m, part : part + 8], None) for n in range(8)]) for m in range(16)]
     for r in range(5):
         outs = small_dft([times(inner[m][r], m * r / 128) for m in range(16)])
         for f in range(16):
@@ -176,7 +192,7 @@
                 y_ref[2 * (128 - e) + 1, pl.ds(top, 8), :] = -im
 
 
-DATA_STEPS = 8
+DATA_STEPS = 4
 
 
 def transform_kernel(data_ref, rider_ref, middle_ref, out_ref, y_ref, *, log_length):
@@ -185,10 +201,12 @@
 
     @pl.when(step < DATA_STEPS)
     def _():
-        block_dft(data_ref, y_ref, pl.multiple_of(step * 8, 8))
+        for part in range(0, data_ref.shape[1], 8):
+            block_dft(data_ref, part, y_ref, pl.multiple_of(step * data_ref.shape[1] + part, 8))
 
     @pl.when(step >= DATA_STEPS)
     def _():
+        products = []
         for q in range(pairs):
             pair = (step - DATA_STEPS) * pairs + q
             cosines = y_ref[2 * pair]
@@ -207,6 +225,10 @@
                 jnp.concatenate([hi, hi, lo], axis=0),
                 preferred_element_type=f32,
             )
+            products.append(z)
+        for q in range(pairs):
+            z = products[q]
+            pair = (step - DATA_STEPS) * pairs + q
             for cls in range(2):
                 zr = z[cls * 64 : cls * 64 + 32]
                 zi = z[cls * 64 + 32 : cls * 64 + 64]
@@ -239,12 +261,13 @@
 
 def transform(data, middle, total_rows):
     pairs = 8
+    rows = data.shape[1] - 8
     return pl.pallas_call(
         functools.partial(transform_kernel, log_length=total_rows.bit_length() - 1),
         grid=(DATA_STEPS + 64 // pairs,),
         in_specs=[
-            pl.BlockSpec((128, 8, LANES), lambda i: (0, jnp.minimum(i, DATA_STEPS - 1), 0)),
-            pl.BlockSpec((128, 8, LANES), lambda i: (0, DATA_STEPS, 0)),
+            pl.BlockSpec((128, rows // DATA_STEPS, LANES), lambda i: (0, jnp.minimum(i, DATA_STEPS - 1), 0)),
+            pl.BlockSpec((128, 8, LANES), lambda i: (0, rows // 8, 0)),
             pl.BlockSpec((pairs, 128, 128), lambda i: (jnp.maximum(i - DATA_STEPS, 0), 0, 0)),
         ],
         out_specs=pl.BlockSpec((128, 2, LANES), lambda i: (0, 0, 0)),
@@ -336,7 +359,7 @@
 
 def finish(gram, root_weight, panel):
     columns, rows = panel.shape
-    width = 512
+    width = 2048
     return pl.pallas_call(
         finish_kernel,
         grid=(rows // width,),
@@ -363,14 +386,7 @@
     columns, rows_dev = panel.shape
     shards = 128
     total_rows = rows_dev * shards
-    slots = samples.shape[1]
-    probability = jax.nn.sigmoid(logits)
-    root_weight = jnp.sqrt(probability * (1.0 - probability))
-    packed = pack(
-        panel,
-        (root_weight * signs.astype(f32))[None, :],
-        jnp.pad(samples, ((0, 0), (0, LANES - slots))),
-    )
+    packed, root_weight = pack(panel, logits[None, :], signs[None, :], samples)
     arrived = lax.all_to_all(packed, AXES, split_axis=0, concat_axis=0, tiled=True)
 
     zero = jnp.minimum(counts[0], 0)
@@ -391,7 +407,7 @@
     gram = lax.all_to_all(
         jnp.broadcast_to(strips[None], (shards, lines, columns)), AXES, split_axis=0, concat_axis=0, tiled=True
     ).reshape(columns, columns)
-    return finish(gram, root_weight[None, :], panel)
+    return finish(gram, root_weight, panel)
 
 
 def solution(mesh):

time: 162 us -> 151 us (0.932)
  Pallas kernels: 41.6 us -> 33.9 us
    pallas_call x1, Pallas kernels: 19.2 us -> 16 us  [transform(): pl.pallas_call(functools.partial(transform_kernel, log_length=total_rows....]
    pallas_call x1, Pallas kernels: 7.05 us -> 4.24 us  [pack(): pl.pallas_call(pack_kernel, grid=(columns // step,), in_specs=[pl.BlockSp...]
    pallas_call x1, Pallas kernels: 15.4 us -> 13.6 us  [finish(): pl.pallas_call(finish_kernel, grid=(rows // width,), in_specs=[pl.BlockSp...]
  transfers between devices with their start and end apart: 2 -> 2, of which waited for: 2 -> 2; matrix products, arithmetic and copies ran while one was open for 12% -> 13% of each run, Pallas kernels for 0% -> 0%
where the time goes in v1:
time: 151 us
  waiting for transfers between devices  46.3 us (31%)
  Pallas kernels  33.9 us (22%)
  blocking collectives  30.5 us (20%)
  other arithmetic  18.7 us (12%)
  starting transfers between devices  18.6 us (12%)
    all_to_all x1, waiting for transfers between devices, on_device(): lax.all_to_all(packed, AXES, split_axis=0, concat_axis=0, tiled=True)  36.2 us
    convert_element_type x1, other arithmetic, rounded_parts(): return (high.astype(bf16), (value - high).astype(bf16))  17.3 us
    pallas_call x1, Pallas kernels, transform(): pl.pallas_call(functools.partial(transform_kernel, log_length=total_rows....  16 us
    all_to_all x1, blocking collectives, on_device(): lax.all_to_all(jnp.broadcast_to(strips[None], (shards, lines, columns)),...  15.2 us
    all_to_all x1, blocking collectives, on_device(): lax.all_to_all(gram_part.reshape(shards, lines, columns), AXES, split_axi...  15.2 us
    pallas_call x1, Pallas kernels, finish(): pl.pallas_call(finish_kernel, grid=(rows // width,), in_specs=[pl.BlockSp...  13.6 us
    all_to_all x1, starting transfers between devices, on_device(): lax.all_to_all(packed, AXES, split_axis=0, concat_axis=0, tiled=True)  11.9 us
    all_to_all x1, waiting for transfers between devices, on_device(): lax.all_to_all(picked, AXES, split_axis=0, concat_axis=0, tiled=True)  10.2 us
  transfers between devices with their start and end apart: 2, of which 2 were waited for; matrix products, arithmetic and copies ran while one was open for 13% of the time, Pallas kernels for 0%

profile of v1, /device:TPU:1, one launch (start us, length us, event | category | flops | bytes accessed | tf_op | source)
XLA Modules:
  0.0 150.6 jit_solution(4900451176224770399)
XLA Ops:
  0.0 4.2 %pack_columns.1 = (f32[128,72,128]{2,1,0:T(8,128)}, f32[1,4096]{1,0:T(1,128)}) custom-call(f32[256,4096]{1,0:T(8,128)} %panel_ref.3, f32[1,4096]{1,0:T(1,128)} %bitcast.10, s32[1,4096]{1,0:T(1,128)} %bitcast.11, s32[1,96]{1,0:T(1,128)} %samples_ref.1), custom_call_target="tpu_custom_call" | custom-call | tf_op jit(solution)/shard_map/pack_columns/pallas_call | solution.py:77
  4.2 11.9 %all-to-all-start = ((f32[128,72,128]{2,1,0:T(8,128)}), f32[128,72,128]{2,1,0:T(8,128)}, u32[]{:S(2)}, u32[]{:S(2)}) async-start(f32[128,72,128]{2,1,0:T(8,128)} %get-tuple-element.7), calls=%async_computation | async-start | bytes 9437184 | tf_op jit(solution)/shard_map/all_to_all | solution.py:390
  16.2 0.1 iota.157
  16.2 0.1 iota.158
  16.3 0.1 iota.153
  16.4 0.1 iota.154
  16.5 0.1 iota.151
  16.6 0.1 iota.148
  17.3 0.1 iota.141
  17.4 0.1 iota.142
  17.5 0.1 iota.138
  17.6 0.1 iota.135
  17.7 0.1 iota.132
  17.8 17.3 %reduce-precision_convert_fusion = (bf16[64,128,64]{2,1,0:T(8,128)(2,1)S(1)}, bf16[64,128,64]{2,1,0:T(8,128)(2,1)S(1)}) fusion(s32[128]{0:T(128)S(1)} %iota.158, pred[64]{0:T(512)(128)(4,1)S(1)} %iota.154, s32[128]{0:T(128)S(1)} %iota.151, s32[128]{0:T(128)S(1)} %iota.148, s32[64]{0:T(128)S(1)} %get-tuple-element.12, s32[64]{0:T(128)S(1)} %get-tuple-element.11, ...), kind=kLoop, calls=%fused_computation.4 | loop fusion | flops 15728640 | bytes 2100480 | tf_op jit(solution)/shard_map/convert_element_type | solution.py:26
  35.1 1.2 pad_maximum_fusion.middle_ref
  36.2 0.0 copy-start
  36.2 36.2 %all-to-all-done.data_ref.rider_ref = f32[128,72,128]{2,1,0:T(8,128)} async-done(((f32[128,72,128]{2,1,0:T(8,128)}), f32[128,72,128]{2,1,0:T(8,128)}, u32[]{:S(2)}, u32[]{:S(2)}) %all-to-all-start) | async-done | bytes 4718624 | tf_op jit(solution)/shard_map/all_to_all | solution.py:390
  72.4 16.0 %sampled_transform.1 = f32[128,2,128]{2,1,0:T(2,128)} custom-call(f32[128,72,128]{2,1,0:T(8,128)} %all-to-all-done.data_ref.rider_ref, f32[128,72,128]{2,1,0:T(8,128)} %all-to-all-done.data_ref.rider_ref, bf16[64,128,128]{2,1,0:T(8,128)(2,1)S(1)} %pad_maximum_fusion.middle_ref), custom_call_target="tpu_custom_call" | custom-call | tf_op jit(solution)/shard_map/sampled_transform/pallas_call | solution.py:265
  88.4 6.7 %all-to-all-start.1 = ((f32[128,2,128]{2,1,0:T(2,128)}), f32[128,2,128]{2,1,0:T(2,128)S(1)}, u32[]{:S(2)}, u32[]{:S(2)}) async-start(f32[128,2,128]{2,1,0:T(2,128)} %sampled_transform.1), calls=%async_computation.1 | async-start | bytes 262144 | tf_op jit(solution)/shard_map/all_to_all | solution.py:397
  95.1 10.2 %all-to-all-done.1 = f32[128,2,128]{2,1,0:T(2,128)S(1)} async-done(((f32[128,2,128]{2,1,0:T(2,128)}), f32[128,2,128]{2,1,0:T(2,128)S(1)}, u32[]{:S(2)}, u32[]{:S(2)}) %all-to-all-start.1) | async-done | bytes 131104 | tf_op jit(solution)/shard_map/all_to_all | solution.py:397
  105.3 0.1 multiply_select_fusion
  105.4 0.4 convolution_select_fusion
  105.8 0.1 reshape.48
  106.0 15.2 %all_to_all.20 = f32[128,2,256]{2,1,0:T(2,128)S(1)} all-to-all(f32[128,2,256]{2,1,0:T(2,128)S(1)} %reshape.48), channel_id=1, replica_groups=mesh['row'=8,'blk'=16] {'row','blk'}, dimensions={0} | all-to-all | bytes 524288 | tf_op jit(solution)/shard_map/all_to_all | solution.py:404
  121.2 0.1 reduce_sum.9
  121.4 0.1 broadcast_in_dim.46
  121.4 15.2 %all_to_all.21 = f32[128,2,256]{2,1,0:T(2,128)S(1)} all-to-all(f32[128,2,256]{2,1,0:T(2,128)S(1)} %broadcast_in_dim.46), channel_id=1, replica_groups=mesh['row'=8,'blk'=16] {'row','blk'}, dimensions={0} | all-to-all | bytes 524288 | tf_op jit(solution)/shard_map/all_to_all | solution.py:407
  136.7 0.2 reshape.49.gram_ref
  136.9 0.0 copy-done
  136.9 13.6 %factor_and_apply.1 = f32[256,4096]{1,0:T(8,128)} custom-call(f32[256,256]{1,0:T(8,128)S(1)} %reshape.49.gram_ref, f32[1,4096]{1,0:T(1,128)S(1)} %copy-done, f32[256,4096]{1,0:T(8,128)} %panel_ref.3), custom_call_target="tpu_custom_call" | custom-call | tf_op jit(solution)/shard_map/factor_and_apply/pallas_call | solution.py:363
  (12 shorter events, 0.1 us)
Async XLA Ops:
  4.2 68.2 %all-to-all-start = ((f32[128,72,128]{2,1,0:T(8,128)}), f32[128,72,128]{2,1,0:T(8,128)}, u32[]{:S(2)}, u32[]{:S(2)}) async-start(f32[128,72,128]{2,1,0:T(8,128)} %get-tuple-element.7), calls=%async_computation | async-start | bytes 9437184 | tf_op jit(solution)/shard_map/all_to_all | solution.py:390
  36.2 100.6 %copy-start = (f32[1,4096]{1,0:T(1,128)S(1)}, f32[1,4096]{1,0:T(1,128)}, u32[]{:S(2)}) copy-start(f32[1,4096]{1,0:T(1,128)} %get-tuple-element.8.root_ref) | copy-start | bytes 49156
  88.4 16.9 %all-to-all-start.1 = ((f32[128,2,128]{2,1,0:T(2,128)}), f32[128,2,128]{2,1,0:T(2,128)S(1)}, u32[]{:S(2)}, u32[]{:S(2)}) async-start(f32[128,2,128]{2,1,0:T(2,128)} %sampled_transform.1), calls=%async_computation.1 | async-start | bytes 262144 | tf_op jit(solution)/shard_map/all_to_all | solution.py:397

commit v2 on v1

--- a/solution.py
+++ b/solution.py
@@ -63,10 +63,11 @@
             tiles = swap_eight([panel_ref[top : top + 8, span] * scale_ref[:, span] for span in spans])
             for i in range(8):
                 line = top + i
-                row = (line % 2) * groups + g
-                out_ref[line // 2, row : row + 8, :] = tiles[i]
+                row = (line // 2) * (2 * groups + 1) + (line % 2) * groups + g
+                out_ref[row : row + 8, :] = tiles[i]
     for q in range(lines // 2):
-        out_ref[q, 2 * groups : 2 * groups + 8, :] = rider_ref[...]
+        row = (q + 1) * (2 * groups + 1) - 1
+        out_ref[row : row + 1, :] = rider_ref[:1]
 
 
 def pack(panel, logits, signs, samples):
@@ -83,9 +84,9 @@
             whole,
             pl.BlockSpec(samples.shape, lambda i: (0, 0)),
         ],
-        out_specs=[pl.BlockSpec((step // 2, 2 * groups + 8, LANES), lambda i: (i, 0, 0)), whole],
+        out_specs=[pl.BlockSpec((step // 2 * (2 * groups + 1), LANES), lambda i: (i, 0)), whole],
         out_shape=[
-            jax.ShapeDtypeStruct((columns // 2, 2 * groups + 8, LANES), f32),
+            jax.ShapeDtypeStruct((columns // 2 * (2 * groups + 1), LANES), f32),
             jax.ShapeDtypeStruct((1, rows), f32),
         ],
         scratch_shapes=[pltpu.VMEM((1, rows), f32), pltpu.VMEM((8, LANES), f32)],
@@ -176,7 +177,7 @@
 
 
 def block_dft(data_ref, part, y_ref, top):
-    inner = [small_dft([(data_ref[16 * n + m, part : part + 8], None) for n in range(8)]) for m in range(16)]
+    inner = [small_dft([(data_ref[(16 * n + m) * 65 + part : (16 * n + m) * 65 + part + 8], None) for n in range(8)]) for m in range(16)]
     for r in range(5):
         outs = small_dft([times(inner[m][r], m * r / 128) for m in range(16)])
         for f in range(16):
@@ -192,17 +193,17 @@
                 y_ref[2 * (128 - e) + 1, pl.ds(top, 8), :] = -im
 
 
-DATA_STEPS = 4
-
-
-def transform_kernel(data_ref, rider_ref, middle_ref, out_ref, y_ref, *, log_length):
+DATA_STEPS = 1
+
+
+def transform_kernel(data_ref, middle_ref, out_ref, y_ref, *, log_length):
     step = pl.program_id(0)
     pairs = middle_ref.shape[0]
 
     @pl.when(step < DATA_STEPS)
     def _():
-        for part in range(0, data_ref.shape[1], 8):
-            block_dft(data_ref, part, y_ref, pl.multiple_of(step * data_ref.shape[1] + part, 8))
+        for part in range(0, 64, 8):
+            block_dft(data_ref, part, y_ref, part)
 
     @pl.when(step >= DATA_STEPS)
     def _():
@@ -244,7 +245,7 @@
                     e = pair
                 else:
                     e = jnp.where(pair == 0, 64, 128 - pair)
-                offset = rider_ref[e].astype(jnp.int32)
+                offset = jnp.broadcast_to(data_ref[pl.ds(e * 65 + 64, 1), :].astype(jnp.int32), (8, LANES))
                 t_hi, t_lo = split_two(sample_phases(offset * 128 + e, log_length))
                 both = jnp.dot(
                     jnp.concatenate([hi, lo], axis=0),
@@ -261,13 +262,11 @@
 
 def transform(data, middle, total_rows):
     pairs = 8
-    rows = data.shape[1] - 8
     return pl.pallas_call(
         functools.partial(transform_kernel, log_length=total_rows.bit_length() - 1),
         grid=(DATA_STEPS + 64 // pairs,),
         in_specs=[
-            pl.BlockSpec((128, rows // DATA_STEPS, LANES), lambda i: (0, jnp.minimum(i, DATA_STEPS - 1), 0)),
-            pl.BlockSpec((128, 8, LANES), lambda i: (0, rows // 8, 0)),
+            pl.BlockSpec(data.shape, lambda i: (0, 0)),
             pl.BlockSpec((pairs, 128, 128), lambda i: (jnp.maximum(i - DATA_STEPS, 0), 0, 0)),
         ],
         out_specs=pl.BlockSpec((128, 2, LANES), lambda i: (0, 0, 0)),
@@ -275,7 +274,7 @@
         scratch_shapes=[pltpu.VMEM((128, 64, LANES), f32)],
         compiler_params=pltpu.CompilerParams(vmem_limit_bytes=48 * 1024 * 1024),
         name="sampled_transform",
-    )(data, data, middle)
+    )(data, middle)
 
 
 def factor_inverse(a_ref, b_ref):
@@ -387,7 +386,9 @@
     shards = 128
     total_rows = rows_dev * shards
     packed, root_weight = pack(panel, logits[None, :], signs[None, :], samples)
-    arrived = lax.all_to_all(packed, AXES, split_axis=0, concat_axis=0, tiled=True)
+    arrived = lax.all_to_all(
+        packed.reshape(shards, 65, 1, LANES), AXES, split_axis=0, concat_axis=0, tiled=True
+    ).reshape(shards * 65, LANES)
 
     zero = jnp.minimum(counts[0], 0)
     m_hi, m_lo = rounded_parts(middle_table(zero))

time: 151 us -> 145 us (0.960)
  waiting for transfers between devices: 46.3 us -> 41.5 us
    all_to_all x1, waiting for transfers between devices: 36.2 us -> 31.3 us  [on_device(): lax.all_to_all(packed.reshape(shards, 65, 1, LANES), AXES, split_axis=0,...]
where the time goes in v2:
time: 145 us
  waiting for transfers between devices  41.5 us (29%)
  Pallas kernels  33.6 us (23%)
  blocking collectives  30.5 us (21%)
  other arithmetic  18.7 us (13%)
  starting transfers between devices  18.1 us (12%)
    all_to_all x1, waiting for transfers between devices, on_device(): lax.all_to_all(packed.reshape(shards, 65, 1, LANES), AXES, split_axis=0,...  31.3 us
    convert_element_type x1, other arithmetic, rounded_parts(): return (high.astype(bf16), (value - high).astype(bf16))  17.3 us
    pallas_call x1, Pallas kernels, transform(): pl.pallas_call(functools.partial(transform_kernel, log_length=total_rows....  15.9 us
    all_to_all x1, blocking collectives, on_device(): lax.all_to_all(gram_part.reshape(shards, lines, columns), AXES, split_axi...  15.3 us
    all_to_all x1, blocking collectives, on_device(): lax.all_to_all(jnp.broadcast_to(strips[None], (shards, lines, columns)),...  15.2 us
    pallas_call x1, Pallas kernels, finish(): pl.pallas_call(finish_kernel, grid=(rows // width,), in_specs=[pl.BlockSp...  13.6 us
    all_to_all x1, starting transfers between devices, on_device(): lax.all_to_all(packed.reshape(shards, 65, 1, LANES), AXES, split_axis=0,...  11.9 us
    all_to_all x1, waiting for transfers between devices, on_device(): lax.all_to_all(picked, AXES, split_axis=0, concat_axis=0, tiled=True)  10.2 us
  transfers between devices with their start and end apart: 2, of which 2 were waited for; matrix products, arithmetic and copies ran while one was open for 13% of the time, Pallas kernels for 0%

profile of v2, /device:TPU:1, one launch (start us, length us, event | category | flops | bytes accessed | tf_op | source)
XLA Modules:
  0.0 145.1 jit_solution(9094990698863802239)
XLA Ops:
  0.0 4.1 %pack_columns.1 = (f32[8320,128]{1,0:T(8,128)}, f32[1,4096]{1,0:T(1,128)}) custom-call(f32[256,4096]{1,0:T(8,128)} %panel_ref.3, f32[1,4096]{1,0:T(1,128)} %bitcast.13, s32[1,4096]{1,0:T(1,128)} %bitcast.14, s32[1,96]{1,0:T(1,128)} %samples_ref.1), custom_call_target="tpu_custom_call" | custom-call | tf_op jit(solution)/shard_map/pack_columns/pallas_call | solution.py:78
  4.1 11.9 %all-to-all-start = ((f32[128,65,1,128]{3,2,1,0:T(1,128)}), f32[128,65,1,128]{3,2,1,0:T(1,128)}, u32[]{:S(2)}, u32[]{:S(2)}) async-start(f32[128,65,1,128]{3,2,1,0:T(1,128)} %bitcast.11), calls=%async_computation | async-start | bytes 8519680 | tf_op jit(solution)/shard_map/all_to_all | solution.py:389
  16.0 0.1 iota.157
  16.1 0.1 iota.158
  16.2 0.1 iota.153
  16.2 0.1 iota.154
  16.3 0.1 iota.151
  16.4 0.1 iota.148
  17.2 0.1 iota.141
  17.2 0.1 iota.142
  17.3 0.1 iota.138
  17.4 0.1 iota.135
  17.5 0.1 iota.132
  17.6 17.3 %reduce-precision_convert_fusion = (bf16[64,128,64]{2,1,0:T(8,128)(2,1)S(1)}, bf16[64,128,64]{2,1,0:T(8,128)(2,1)S(1)}) fusion(s32[128]{0:T(128)S(1)} %iota.158, pred[64]{0:T(512)(128)(4,1)S(1)} %iota.154, s32[128]{0:T(128)S(1)} %iota.151, s32[128]{0:T(128)S(1)} %iota.148, s32[64]{0:T(128)S(1)} %get-tuple-element.12, s32[64]{0:T(128)S(1)} %get-tuple-element.11, ...), kind=kLoop, calls=%fused_computation.4 | loop fusion | flops 15728640 | bytes 2100480 | tf_op jit(solution)/shard_map/convert_element_type | solution.py:26
  34.9 1.2 pad_maximum_fusion.middle_ref
  36.1 31.3 %all-to-all-done = f32[128,65,1,128]{3,2,1,0:T(1,128)} async-done(((f32[128,65,1,128]{3,2,1,0:T(1,128)}), f32[128,65,1,128]{3,2,1,0:T(1,128)}, u32[]{:S(2)}, u32[]{:S(2)}) %all-to-all-start) | async-done | bytes 4259872 | tf_op jit(solution)/shard_map/all_to_all | solution.py:389
  67.4 0.0 copy-start
  67.4 15.9 %sampled_transform.1 = f32[128,2,128]{2,1,0:T(2,128)} custom-call(f32[8320,128]{1,0:T(8,128)} %bitcast.4.data_ref, bf16[64,128,128]{2,1,0:T(8,128)(2,1)S(1)} %pad_maximum_fusion.middle_ref), custom_call_target="tpu_custom_call" | custom-call | tf_op jit(solution)/shard_map/sampled_transform/pallas_call | solution.py:265
  83.4 6.2 %all-to-all-start.1 = ((f32[128,2,128]{2,1,0:T(2,128)}), f32[128,2,128]{2,1,0:T(2,128)S(1)}, u32[]{:S(2)}, u32[]{:S(2)}) async-start(f32[128,2,128]{2,1,0:T(2,128)} %sampled_transform.1), calls=%async_computation.1 | async-start | bytes 262144 | tf_op jit(solution)/shard_map/all_to_all | solution.py:398
  89.5 10.2 %all-to-all-done.1 = f32[128,2,128]{2,1,0:T(2,128)S(1)} async-done(((f32[128,2,128]{2,1,0:T(2,128)}), f32[128,2,128]{2,1,0:T(2,128)S(1)}, u32[]{:S(2)}, u32[]{:S(2)}) %all-to-all-start.1) | async-done | bytes 131104 | tf_op jit(solution)/shard_map/all_to_all | solution.py:398
  99.7 0.1 multiply_select_fusion
  99.8 0.4 convolution_select_fusion
  100.2 0.1 reshape.56
  100.4 15.3 %all_to_all.20 = f32[128,2,256]{2,1,0:T(2,128)S(1)} all-to-all(f32[128,2,256]{2,1,0:T(2,128)S(1)} %reshape.56), channel_id=1, replica_groups=mesh['row'=8,'blk'=16] {'row','blk'}, dimensions={0} | all-to-all | bytes 524288 | tf_op jit(solution)/shard_map/all_to_all | solution.py:405
  115.6 0.1 reduce_sum.9
  115.8 0.1 broadcast_in_dim.46
  115.8 15.2 %all_to_all.21 = f32[128,2,256]{2,1,0:T(2,128)S(1)} all-to-all(f32[128,2,256]{2,1,0:T(2,128)S(1)} %broadcast_in_dim.46), channel_id=1, replica_groups=mesh['row'=8,'blk'=16] {'row','blk'}, dimensions={0} | all-to-all | bytes 524288 | tf_op jit(solution)/shard_map/all_to_all | solution.py:408
  131.1 0.2 reshape.57.gram_ref
  131.3 0.0 copy-done
  131.3 13.6 %factor_and_apply.1 = f32[256,4096]{1,0:T(8,128)} custom-call(f32[256,256]{1,0:T(8,128)S(1)} %reshape.57.gram_ref, f32[1,4096]{1,0:T(1,128)S(1)} %copy-done, f32[256,4096]{1,0:T(8,128)} %panel_ref.3), custom_call_target="tpu_custom_call" | custom-call | tf_op jit(solution)/shard_map/factor_and_apply/pallas_call | solution.py:362
  (12 shorter events, 0.1 us)
Async XLA Ops:
  4.1 63.3 %all-to-all-start = ((f32[128,65,1,128]{3,2,1,0:T(1,128)}), f32[128,65,1,128]{3,2,1,0:T(1,128)}, u32[]{:S(2)}, u32[]{:S(2)}) async-start(f32[128,65,1,128]{3,2,1,0:T(1,128)} %bitcast.11), calls=%async_computation | async-start | bytes 8519680 | tf_op jit(solution)/shard_map/all_to_all | solution.py:389
  67.4 63.9 %copy-start = (f32[1,4096]{1,0:T(1,128)S(1)}, f32[1,4096]{1,0:T(1,128)}, u32[]{:S(2)}) copy-start(f32[1,4096]{1,0:T(1,128)} %get-tuple-element.8.root_ref) | copy-start | bytes 49156
  83.4 16.4 %all-to-all-start.1 = ((f32[128,2,128]{2,1,0:T(2,128)}), f32[128,2,128]{2,1,0:T(2,128)S(1)}, u32[]{:S(2)}, u32[]{:S(2)}) async-start(f32[128,2,128]{2,1,0:T(2,128)} %sampled_transform.1), calls=%async_computation.1 | async-start | bytes 262144 | tf_op jit(solution)/shard_map/all_to_all | solution.py:398

commit v3 on v2

--- a/solution.py
+++ b/solution.py
@@ -279,18 +279,18 @@
 
 def factor_inverse(a_ref, b_ref):
     size = a_ref.shape[0]
-    block = 32
+    block = 64
     line = lax.broadcasted_iota(jnp.int32, (8, LANES), 0)
     spread = lambda row: jnp.broadcast_to(row, (8, LANES))
     for lo in range(0, size, block):
         home = lo // LANES
         off = lo % LANES
         spots = [(a_ref, g) for g in range(home, size // LANES)] + [(b_ref, g) for g in range(home + 1)]
-        rows = [[ref[lo + 8 * v : lo + 8 * v + 8, g * LANES : (g + 1) * LANES] for ref, g in spots] for v in range(4)]
+        rows = [[ref[lo + 8 * v : lo + 8 * v + 8, g * LANES : (g + 1) * LANES] for ref, g in spots] for v in range(block // 8)]
         pivots = []
-        for t in range(4):
+        for t in range(block // 8):
             col = [
-                {v: jnp.broadcast_to(rows[v][0][:, off + 8 * t + j : off + 8 * t + j + 1], (8, LANES)) for v in range(t, 4)}
+                {v: jnp.broadcast_to(rows[v][0][:, off + 8 * t + j : off + 8 * t + j + 1], (8, LANES)) for v in range(t, block // 8)}
                 for j in range(8)
             ]
             diag = jnp.ones((8, LANES), f32)
@@ -298,23 +298,23 @@
                 pivot = spread(col[j][t][j : j + 1])
                 inverse = 1.0 / pivot
                 diag = jnp.where(line == j, pivot, diag)
-                mult = {v: col[j][v] * inverse for v in range(t, 4)}
+                mult = {v: col[j][v] * inverse for v in range(t, block // 8)}
                 mult[t] = jnp.where(line > j, mult[t], 0.0)
                 for n in range(j + 1, 8):
                     across = spread(col[j][t][n : n + 1])
-                    for v in range(t, 4):
+                    for v in range(t, block // 8):
                         col[n][v] = col[n][v] - mult[v] * across
                 for g in range(len(spots)):
                     across = spread(rows[t][g][j : j + 1])
-                    for v in range(t, 4):
+                    for v in range(t, block // 8):
                         rows[v][g] = rows[v][g] - mult[v] * across
             pivots.append(diag)
-        for v in range(4):
+        for v in range(block // 8):
             scale = lax.rsqrt(pivots[v])
             scale = scale * (1.5 - 0.5 * (pivots[v] * scale) * scale)
             rows[v] = [part * scale for part in rows[v]]
         n_a = size // LANES - home
-        for v in range(4):
+        for v in range(block // 8):
             for g in range(home + 1):
                 b_ref[lo + 8 * v : lo + 8 * v + 8, g * LANES : (g + 1) * LANES] = rows[v][n_a + g]
         if lo + block == size:
@@ -330,14 +330,17 @@
             b_ref[top:end, : (home + 1) * LANES] = b_ref[top:end, : (home + 1) * LANES] - change[:, n_a * LANES :]
 
 
-def finish_kernel(gram_ref, root_ref, panel_ref, out_ref, a_ref, b_ref, w_ref, held_ref, sem):
+def finish_kernel(gram_ref, high_ref, low_ref, out_ref, a_ref, b_ref, w_ref, held_ref, sems):
     size = gram_ref.shape[0]
     width = out_ref.shape[1]
 
     @pl.when(pl.program_id(0) == 0)
     def _():
-        fetch = pltpu.make_async_copy(panel_ref, held_ref, sem)
-        fetch.start()
+        fetches = [
+            pltpu.make_async_copy(source, held_ref.at[k], sems.at[k]) for k, source in enumerate((high_ref, low_ref))
+        ]
+        for fetch in fetches:
+            fetch.start()
         a_ref[...] = gram_ref[...]
         b_ref[...] = (
             lax.broadcasted_iota(jnp.int32, (size, size), 0) == lax.broadcasted_iota(jnp.int32, (size, size), 1)
@@ -349,22 +352,23 @@
         w_ref[:, :size] = high
         w_ref[:, size : 2 * size] = high
         w_ref[:, 2 * size :] = low
-        fetch.wait()
+        for fetch in fetches:
+            fetch.wait()
 
     span = pl.ds(pl.multiple_of(pl.program_id(0) * width, width), width)
-    high, low = split_two(held_ref[:, span] * root_ref[...])
+    high, low = held_ref[0, :, span], held_ref[1, :, span]
     out_ref[...] = jnp.dot(w_ref[...], jnp.concatenate([high, low, high], axis=0), preferred_element_type=f32)
 
 
-def finish(gram, root_weight, panel):
-    columns, rows = panel.shape
+def finish(gram, high, low):
+    columns, rows = high.shape
     width = 2048
     return pl.pallas_call(
         finish_kernel,
         grid=(rows // width,),
         in_specs=[
             pl.BlockSpec((columns, columns), lambda i: (0, 0)),
-            pl.BlockSpec((1, width), lambda i: (0, i)),
+            pl.BlockSpec(memory_space=pl.ANY),
             pl.BlockSpec(memory_space=pl.ANY),
         ],
         out_specs=pl.BlockSpec((columns, width), lambda i: (0, i)),
@@ -373,12 +377,12 @@
             pltpu.VMEM((columns, columns), f32),
             pltpu.VMEM((columns, columns), f32),
             pltpu.VMEM((columns, 3 * columns), bf16),
-            pltpu.VMEM((columns, rows), f32),
-            pltpu.SemaphoreType.DMA,
+            pltpu.VMEM((2, columns, rows), bf16),
+            pltpu.SemaphoreType.DMA((2,)),
         ],
         compiler_params=pltpu.CompilerParams(vmem_limit_bytes=48 * 1024 * 1024),
         name="factor_and_apply",
-    )(gram, root_weight, pltpu.with_memory_space_constraint(panel, pltpu.HBM))
+    )(gram, *(pltpu.with_memory_space_constraint(part, pltpu.HBM) for part in (high, low)))
 
 
 def on_device(panel, logits, signs, samples, counts):
@@ -408,7 +412,7 @@
     gram = lax.all_to_all(
         jnp.broadcast_to(strips[None], (shards, lines, columns)), AXES, split_axis=0, concat_axis=0, tiled=True
     ).reshape(columns, columns)
-    return finish(gram, root_weight, panel)
+    return finish(gram, *rounded_parts(panel * root_weight))
 
 
 def solution(mesh):

time: 145 us -> 146 us (level)
  blocking collectives: 30.5 us -> 15.3 us
  waiting for transfers between devices: 41.5 us -> 48 us
  other arithmetic: 18.7 us -> 23.7 us
  starting transfers between devices: 18.1 us -> 22.1 us
    all_to_all x1 -> x0, blocking collectives: 15.2 us -> none  [on_device(): lax.all_to_all(jnp.broadcast_to(strips[None], (shards, lines, columns)),...]
    all_to_all x0 -> x1, waiting for transfers between devices: none -> 6.54 us  [on_device(): lax.all_to_all(jnp.broadcast_to(strips[None], (shards, lines, columns)),...]
    convert_element_type x1 -> x2, other arithmetic: 17.3 us -> 22.3 us  [rounded_parts(): return (high.astype(bf16), (value - high).astype(bf16))]
    all_to_all x0 -> x1, starting transfers between devices: none -> 3.99 us  [on_device(): lax.all_to_all(jnp.broadcast_to(strips[None], (shards, lines, columns)),...]
  transfers between devices with their start and end apart: 2 -> 3, of which waited for: 2 -> 3; matrix products, arithmetic and copies ran while one was open for 13% -> 17% of each run, Pallas kernels for 0% -> 0%
where the time goes in v3:
time: 146 us
  waiting for transfers between devices  48 us (33%)
  Pallas kernels  33.2 us (23%)
  other arithmetic  23.7 us (16%)
  starting transfers between devices  22.1 us (15%)
  blocking collectives  15.3 us (10%)
  local copies, waits for them, and re-layouts  2.03 us (1%)
    all_to_all x1, waiting for transfers between devices, on_device(): lax.all_to_all(packed.reshape(shards, 65, 1, LANES), AXES, split_axis=0,...  31.3 us
    convert_element_type x2, other arithmetic, rounded_parts(): return (high.astype(bf16), (value - high).astype(bf16))  22.3 us
    pallas_call x1, Pallas kernels, transform(): pl.pallas_call(functools.partial(transform_kernel, log_length=total_rows....  15.9 us
    all_to_all x1, blocking collectives, on_device(): lax.all_to_all(gram_part.reshape(shards, lines, columns), AXES, split_axi...  15.3 us
    pallas_call x1, Pallas kernels, finish(): pl.pallas_call(finish_kernel, grid=(rows // width,), in_specs=[pl.BlockSp...  13.2 us
    all_to_all x1, starting transfers between devices, on_device(): lax.all_to_all(packed.reshape(shards, 65, 1, LANES), AXES, split_axis=0,...  11.9 us
    all_to_all x1, waiting for transfers between devices, on_device(): lax.all_to_all(picked, AXES, split_axis=0, concat_axis=0, tiled=True)  10.2 us
    all_to_all x1, waiting for transfers between devices, on_device(): lax.all_to_all(jnp.broadcast_to(strips[None], (shards, lines, columns)),...  6.54 us
  transfers between devices with their start and end apart: 3, of which 3 were waited for; matrix products, arithmetic and copies ran while one was open for 17% of the time, Pallas kernels for 0%

profile of v3, /device:TPU:1, one launch (start us, length us, event | category | flops | bytes accessed | tf_op | source)
XLA Modules:
  0.0 145.6 jit_solution(6412607185579762124)
XLA Ops:
  0.0 4.1 %pack_columns.1 = (f32[8320,128]{1,0:T(8,128)}, f32[1,4096]{1,0:T(1,128)}) custom-call(f32[256,4096]{1,0:T(8,128)} %panel_ref.1, f32[1,4096]{1,0:T(1,128)} %bitcast.14, s32[1,4096]{1,0:T(1,128)} %bitcast.15, s32[1,96]{1,0:T(1,128)} %samples_ref.1), custom_call_target="tpu_custom_call" | custom-call | tf_op jit(solution)/shard_map/pack_columns/pallas_call | solution.py:78
  4.1 11.9 %all-to-all-start = ((f32[128,65,1,128]{3,2,1,0:T(1,128)}), f32[128,65,1,128]{3,2,1,0:T(1,128)}, u32[]{:S(2)}, u32[]{:S(2)}) async-start(f32[128,65,1,128]{3,2,1,0:T(1,128)} %bitcast.12), calls=%async_computation | async-start | bytes 8519680 | tf_op jit(solution)/shard_map/all_to_all | solution.py:393
  16.0 0.1 iota.157
  16.1 0.1 iota.158
  16.2 0.1 iota.153
  16.2 0.1 iota.154
  16.3 0.1 iota.151
  16.4 0.1 iota.148
  17.2 0.1 iota.141
  17.2 0.1 iota.142
  17.3 0.1 iota.138
  17.4 0.1 iota.135
  17.5 0.1 iota.132
  17.6 17.3 %reduce-precision_convert_fusion.1 = (bf16[64,128,64]{2,1,0:T(8,128)(2,1)S(1)}, bf16[64,128,64]{2,1,0:T(8,128)(2,1)S(1)}) fusion(s32[128]{0:T(128)S(1)} %iota.158, pred[64]{0:T(512)(128)(4,1)S(1)} %iota.154, s32[128]{0:T(128)S(1)} %iota.151, s32[128]{0:T(128)S(1)} %iota.148, s32[64]{0:T(128)S(1)} %get-tuple-element.14, s32[64]{0:T(128)S(1)} %get-tuple-element.13, ...), kind=kLoop, calls=%fused_computation.6 | loop fusion | flops 15728640 | bytes 2100480 | tf_op jit(solution)/shard_map/convert_element_type | solution.py:26
  34.9 1.2 pad_maximum_fusion.middle_ref
  36.1 31.3 %all-to-all-done = f32[128,65,1,128]{3,2,1,0:T(1,128)} async-done(((f32[128,65,1,128]{3,2,1,0:T(1,128)}), f32[128,65,1,128]{3,2,1,0:T(1,128)}, u32[]{:S(2)}, u32[]{:S(2)}) %all-to-all-start) | async-done | bytes 4259872 | tf_op jit(solution)/shard_map/all_to_all | solution.py:393
  67.4 0.0 copy-start
  67.4 15.9 %sampled_transform.1 = f32[128,2,128]{2,1,0:T(2,128)} custom-call(f32[8320,128]{1,0:T(8,128)} %bitcast.4.data_ref, bf16[64,128,128]{2,1,0:T(8,128)(2,1)S(1)} %pad_maximum_fusion.middle_ref), custom_call_target="tpu_custom_call" | custom-call | tf_op jit(solution)/shard_map/sampled_transform/pallas_call | solution.py:265
  83.3 6.2 %all-to-all-start.1 = ((f32[128,2,128]{2,1,0:T(2,128)}), f32[128,2,128]{2,1,0:T(2,128)S(1)}, u32[]{:S(2)}, u32[]{:S(2)}) async-start(f32[128,2,128]{2,1,0:T(2,128)} %sampled_transform.1), calls=%async_computation.1 | async-start | bytes 262144 | tf_op jit(solution)/shard_map/all_to_all | solution.py:402
  89.5 10.2 %all-to-all-done.1 = f32[128,2,128]{2,1,0:T(2,128)S(1)} async-done(((f32[128,2,128]{2,1,0:T(2,128)}), f32[128,2,128]{2,1,0:T(2,128)S(1)}, u32[]{:S(2)}, u32[]{:S(2)}) %all-to-all-start.1) | async-done | bytes 131104 | tf_op jit(solution)/shard_map/all_to_all | solution.py:402
  99.7 0.1 multiply_select_fusion
  99.8 0.4 convolution_select_fusion
  100.2 0.1 reshape.56
  100.3 15.3 %all_to_all.20 = f32[128,2,256]{2,1,0:T(2,128)S(1)} all-to-all(f32[128,2,256]{2,1,0:T(2,128)S(1)} %reshape.56), channel_id=1, replica_groups=mesh['row'=8,'blk'=16] {'row','blk'}, dimensions={0} | all-to-all | bytes 524288 | tf_op jit(solution)/shard_map/all_to_all | solution.py:409
  115.6 0.1 reduce_sum.9
  115.8 0.8 broadcast_in_dim.46
  116.5 4.0 %all-to-all-start.3 = ((f32[128,2,256]{2,1,0:T(2,128)}), f32[128,2,256]{2,1,0:T(2,128)S(1)}, u32[]{:S(2)}, u32[]{:S(2)}) async-start(f32[128,2,256]{2,1,0:T(2,128)} %broadcast_in_dim.46), calls=%async_computation.3 | async-start | bytes 524288 | tf_op jit(solution)/shard_map/all_to_all | solution.py:412
  120.5 0.0 copy-done
  120.5 5.0 %fusion.1 = (bf16[256,4096]{1,0:T(8,128)(2,1)}, bf16[256,4096]{1,0:T(8,128)(2,1)}) fusion(f32[256,4096]{1,0:T(8,128)} %panel_ref.1, f32[4096]{0:T(1024)S(1)} %bitcast.16), kind=kLoop, calls=%fused_computation.8 | loop fusion | flops 5242880 | bytes 8404992 | tf_op jit(solution)/shard_map/convert_element_type | solution.py:26
  125.5 6.5 %all-to-all-done.3 = f32[128,2,256]{2,1,0:T(2,128)S(1)} async-done(((f32[128,2,256]{2,1,0:T(2,128)}), f32[128,2,256]{2,1,0:T(2,128)S(1)}, u32[]{:S(2)}, u32[]{:S(2)}) %all-to-all-start.3) | async-done | bytes 262176 | tf_op jit(solution)/shard_map/all_to_all | solution.py:412
  132.0 0.2 reshape.57.gram_ref
  132.2 13.2 %factor_and_apply.1 = f32[256,4096]{1,0:T(8,128)} custom-call(f32[256,256]{1,0:T(8,128)S(1)} %reshape.57.gram_ref, bf16[256,4096]{1,0:T(8,128)(2,1)} %get-tuple-element.10.high_ref, bf16[256,4096]{1,0:T(8,128)(2,1)} %get-tuple-element.9.low_ref), custom_call_target="tpu_custom_call" | custom-call | tf_op jit(solution)/shard_map/factor_and_apply/pallas_call | solution.py:366
  (12 shorter events, 0.1 us)
Async XLA Ops:
  4.1 63.3 %all-to-all-start = ((f32[128,65,1,128]{3,2,1,0:T(1,128)}), f32[128,65,1,128]{3,2,1,0:T(1,128)}, u32[]{:S(2)}, u32[]{:S(2)}) async-start(f32[128,65,1,128]{3,2,1,0:T(1,128)} %bitcast.12), calls=%async_computation | async-start | bytes 8519680 | tf_op jit(solution)/shard_map/all_to_all | solution.py:393
  67.4 53.1 %copy-start = (f32[1,4096]{1,0:T(1,128)S(1)}, f32[1,4096]{1,0:T(1,128)}, u32[]{:S(2)}) copy-start(f32[1,4096]{1,0:T(1,128)} %get-tuple-element.8) | copy-start | bytes 49156
  83.3 16.4 %all-to-all-start.1 = ((f32[128,2,128]{2,1,0:T(2,128)}), f32[128,2,128]{2,1,0:T(2,128)S(1)}, u32[]{:S(2)}, u32[]{:S(2)}) async-start(f32[128,2,128]{2,1,0:T(2,128)} %sampled_transform.1), calls=%async_computation.1 | async-start | bytes 262144 | tf_op jit(solution)/shard_map/all_to_all | solution.py:402
  116.5 15.5 %all-to-all-start.3 = ((f32[128,2,256]{2,1,0:T(2,128)}), f32[128,2,256]{2,1,0:T(2,128)S(1)}, u32[]{:S(2)}, u32[]{:S(2)}) async-start(f32[128,2,256]{2,1,0:T(2,128)} %broadcast_in_dim.46), calls=%async_computation.3 | async-start | bytes 524288 | tf_op jit(solution)/shard_map/all_to_all | solution.py:412
